TPU v7x, 32 devices: a whole 2x2x4 slice. The times are simulated.
32 devices in a mesh: frame: 4 (over y, x), tile: 8 (over z, core).
Axes of the slice: x: 2, y: 2, z: 4, core: 2. Of those that a mesh axis runs over, the one named last changes fastest.
Arguments:
- saved_codes: bfloat16 [8, 32, 32, 128], P('frame', 'tile'), may hold values from -1 to 1
- saved_scales: float32 [8, 32, 32], P('frame', 'tile'), may hold values from 0.5 to 2.5
- kernels: bfloat16 [2, 27, 128, 128], replicated, may hold values from -0.109375 to 0.109375
- norm_gains: float32 [2, 128], replicated, may hold values from 0.25 to 1.75
- cotangent: bfloat16 [8, 32, 32, 128], P('frame', 'tile'), may hold values from -13 to 13
Outputs:
- input_grad: bfloat16 [8, 32, 32, 128], P('frame', 'tile')
- kernel_grads: float32 [54, 128, 128], P(None, 'tile', 'frame')
All inputs are finite; a program needn't handle non-finite values.
Results may differ from a plain program's by a relative error of at most 0.028.
Values may be sent and summed in bfloat16 or wider, within the bound.
A program may use at most 64 MiB of HBM per device.

v0:
```python
import math

import jax
import jax.numpy as jnp
from jax import lax
from jax.sharding import PartitionSpec as P

EPS = 1e-06


def from_behind(value, axis, steps):
    count = lax.axis_size(axis)
    first, last = (max(0, -steps), min(count, count - steps))
    return lax.ppermute(value, axis, [(source, source + steps) for source in range(first, last)])


def with_halo(cells, sides, width):
    for axis, dim in sides:
        count = lax.axis_size(axis)
        ends = count - 1
        head = lax.slice_in_dim(cells, 0, width, axis=dim)
        tail = lax.slice_in_dim(cells, cells.shape[dim] - width, cells.shape[dim], axis=dim)
        cells = jnp.concatenate(
            [
                lax.ppermute(tail, axis, [(i, (i + 1) % count) for i in range(ends)]),
                cells,
                lax.ppermute(head, axis, [((i + 1) % count, i) for i in range(ends)]),
            ],
            axis=dim,
        )
    return cells


def patches(extended, frames, rows, columns, offset, sign):
    pieces = []
    for depth in range(3):
        for down in range(3):
            for across in range(3):
                first_frame = offset + sign * depth
                first_row = 1 + sign * (down - 1) + (offset - 2 * (sign < 0) * 0) * 0
                first_col = 1 + sign * (across - 1)
                pieces.append(
                    extended[
                        first_frame : first_frame + frames,
                        first_row : first_row + rows,
                        first_col : first_col + columns,
                    ]
                )
    joined = jnp.concatenate(pieces, axis=-1)
    return joined.reshape(frames * rows * columns, joined.shape[-1])


def pad_columns(block):
    return jnp.pad(block, ((0, 0), (0, 0), (1, 1), (0, 0)))


def extend_input(layer_in):
    earlier = from_behind(layer_in, "frame", 1)
    joined = jnp.concatenate([earlier, layer_in], axis=0)
    widened = with_halo(joined, (("tile", 1),), 1)
    return pad_columns(widened)


def extend_cotangent(pre_grad):
    later = from_behind(pre_grad, "frame", -1)
    joined = jnp.concatenate([pre_grad, later], axis=0)
    widened = with_halo(joined, (("tile", 1),), 1)
    return pad_columns(widened)


def local(saved_codes, saved_scales, kernels, norm_gains, cotangent):
    frames, rows, columns, channels = saved_codes.shape
    layer_count = kernels.shape[0]
    cells = frames * rows * columns
    layer_in = (saved_codes.astype(jnp.float32) * saved_scales[..., None]).astype(jnp.bfloat16)
    extended_list = []
    states = []
    for layer in range(layer_count):
        extended = extend_input(layer_in)
        extended_list.append(extended)
        columns_in = patches(extended, frames, rows, columns, 0, 1)
        forward_kernel = kernels[layer].reshape(27 * channels, channels)
        pre_norm = jnp.dot(columns_in, forward_kernel, preferred_element_type=jnp.float32)
        inverse = lax.rsqrt(jnp.mean(pre_norm * pre_norm, axis=-1, keepdims=True) + EPS)
        normed = pre_norm * inverse * norm_gains[layer]
        states.append((pre_norm, inverse, normed))
        if layer + 1 < layer_count:
            layer_in = (
                jax.nn.silu(normed).astype(jnp.bfloat16).reshape(frames, rows, columns, channels)
            )
    upstream = cotangent.reshape(cells, channels)
    grads_list = [None] * layer_count
    for layer in reversed(range(layer_count)):
        pre_norm, inverse, normed = states[layer]
        sigma = jax.nn.sigmoid(normed)
        scaled = (
            norm_gains[layer]
            * upstream.astype(jnp.float32)
            * sigma
            * (1.0 + normed * (1.0 - sigma))
        )
        mixed = jnp.mean(pre_norm * scaled, axis=-1, keepdims=True)
        pre_grad = (inverse * scaled - pre_norm * inverse**3 * mixed).astype(jnp.bfloat16)
        columns_in = patches(extended_list[layer], frames, rows, columns, 0, 1)
        kernel_part = lax.dot_general(
            columns_in, pre_grad, (((0,), (0,)), ((), ())), preferred_element_type=jnp.float32
        )
        grads_list[layer] = kernel_part.reshape(27, channels, channels)
        spread_grad = extend_cotangent(pre_grad.reshape(frames, rows, columns, channels))
        columns_back = patches(spread_grad, frames, rows, columns, 2, -1)
        back_kernel = jnp.transpose(kernels[layer], (0, 2, 1)).reshape(27 * channels, channels)
        upstream = jnp.dot(columns_back, back_kernel, preferred_element_type=jnp.float32).astype(
            jnp.bfloat16
        )
    input_grad = upstream.reshape(frames, rows, columns, channels)
    stacked = jnp.concatenate(grads_list, axis=0)
    partial_sum = lax.psum_scatter(
        stacked.astype(jnp.bfloat16), "tile", scatter_dimension=1, tiled=True
    )
    summed = lax.psum_scatter(partial_sum, "frame", scatter_dimension=2, tiled=True).astype(
        jnp.float32
    )
    total_cells = cells * lax.axis_size("frame") * lax.axis_size("tile")
    kernel_grads = summed / jnp.float32(math.sqrt(total_cells))
    return (input_grad, kernel_grads)


def solution(mesh):
    in_specs = (
        P("frame", "tile", None, None),
        P("frame", "tile", None),
        P(),
        P(),
        P("frame", "tile", None, None),
    )
    out_specs = (P("frame", "tile", None, None), P(None, "tile", "frame"))
    return jax.shard_map(local, mesh=mesh, in_specs=in_specs, out_specs=out_specs, check_vma=False)
```

profile of v0, /device:TPU:0, one launch (start us, length us, event | category | flops | bytes accessed | tf_op | source)
XLA Modules:
  0.0 143.5 jit_solution(338652537655023398)
XLA Ops:
  7.2 0.9 multiply_convert_fusion.1
  8.2 4.9 %collective-permute-start = (bf16[2,4,32,128]{3,2,1,0:T(8,128)(2,1)S(1)}, bf16[2,4,32,128]{3,2,1,0:T(8,128)(2,1)S(1)}, u32[]{:S(2)}, u32[]{:S(2)}) collective-permute-start(bf16[2,4,32,128]{3,2,1,0:T(8,128)(2,1)S(1)} %multiply_convert_fusion.1), channel_id=1, source_target_pairs={{0,8},{8,16},{16,24},{1,9},{9,17},{17,25},{2,10},{10,18},{18,26},{... | collective-permute-start | bytes 196616 | tf_op jit(solution)/shard_map/ppermute | solution.py:14
  13.0 3.2 %slice_bitcast_fusion.3 = (bf16[27,128,128]{1,2,0:T(8,128)(2,1)S(1)}, bf16[27,128,128]{1,2,0:T(8,128)(2,1)S(1)}, bf16[1,27,128,128]{3,2,1,0:T(8,128)(2,1)}, bf16[1,27,128,128]{3,2,1,0:T(8,128)(2,1)S(1)}) fusion(bf16[2,27,128,128]{3,2,1,0:T(8,128)(2,1)} %param.7), kind=kLoop, calls=%fused_computation.191 | loop fusion | bytes 5308416 | tf_op jit(solution)/shard_map/transpose | solution.py:111
  16.3 1.5 %collective-permute-start.1 = (bf16[4,1,32,128]{3,2,1,0:T(8,128)(2,1)S(1)}, bf16[4,1,32,128]{3,2,1,0:T(8,128)(2,1)S(1)}, u32[]{:S(2)}, u32[]{:S(2)}) collective-permute-start(bf16[4,1,32,128]{3,2,1,0:T(8,128)(2,1)S(1)} %get-tuple-element.100), channel_id=1, source_target_pairs={{0,1},{1,2},{2,3},{3,4},{4,5},{5,6},{6,7},{8,9},{9,10},{10,11},{11... | collective-permute-start | bytes 98312 | tf_op jit(solution)/shard_map/ppermute | solution.py:25
  17.8 1.3 collective-permute-start.2
  19.1 3.4 %collective-permute-done.2 = bf16[4,1,32,128]{3,2,1,0:T(8,128)(2,1)S(1)} collective-permute-done((bf16[4,1,32,128]{3,2,1,0:T(8,128)(2,1)S(1)}, bf16[4,1,32,128]{3,2,1,0:T(8,128)(2,1)S(1)}, u32[]{:S(2)}, u32[]{:S(2)}) %collective-permute-start.2) | collective-permute-done | bytes 32800 | tf_op jit(solution)/shard_map/ppermute | solution.py:27
  23.7 0.7 multiply_reduce_fusion.3
  24.4 0.6 copy-done.2
  25.1 0.7 multiply_convert_fusion
  25.8 4.0 %collective-permute-start.3 = (bf16[2,4,32,128]{3,2,1,0:T(8,128)(2,1)}, bf16[2,4,32,128]{3,2,1,0:T(8,128)(2,1)}, u32[]{:S(2)}, u32[]{:S(2)}) collective-permute-start(bf16[2,4,32,128]{3,2,1,0:T(8,128)(2,1)} %bitcast.3), channel_id=1, source_target_pairs={{0,8},{8,16},{16,24},{1,9},{9,17},{17,25},{2,10},{10,18},{18,26},{... | collective-permute-start | bytes 196616 | tf_op jit(solution)/shard_map/ppermute | solution.py:14
  29.8 1.6 %copy.20 = bf16[27,128,128]{2,1,0:T(8,128)(2,1)} copy(bf16[27,128,128]{1,2,0:T(8,128)(2,1)S(1)} %get-tuple-element.11) | data formatting | bytes 1769472 | tf_op jit(solution)/shard_map/transpose | solution.py:111
  31.5 1.6 %copy.21 = bf16[27,128,128]{2,1,0:T(8,128)(2,1)} copy(bf16[27,128,128]{1,2,0:T(8,128)(2,1)S(1)} %get-tuple-element.10) | data formatting | bytes 1769472 | tf_op jit(solution)/shard_map/transpose | solution.py:111
  33.1 0.9 copy.22
  34.0 0.8 pad_maximum_fusion.14
  34.8 4.2 %collective-permute-start.4 = (bf16[4,1,32,128]{3,2,1,0:T(8,128)(2,1)S(1)}, bf16[4,1,32,128]{3,2,1,0:T(8,128)(2,1)S(1)}, u32[]{:S(2)}, u32[]{:S(2)}) collective-permute-start(bf16[4,1,32,128]{3,2,1,0:T(8,128)(2,1)S(1)} %get-tuple-element.96), channel_id=1, source_target_pairs={{0,1},{1,2},{2,3},{3,4},{4,5},{5,6},{6,7},{8,9},{9,10},{10,11},{11... | collective-permute-start | bytes 98312 | tf_op jit(solution)/shard_map/ppermute | solution.py:25
  39.0 1.3 collective-permute-start.5
  40.3 0.8 pad_maximum_fusion.7
  41.1 1.0 collective-permute-done.5
  42.1 1.0 fusion.25
  43.3 1.0 pad_maximum_fusion.2
  44.5 0.9 constant_dynamic-update-slice_fusion.49
  46.0 2.2 %copy.23 = bf16[3456,256]{1,0:T(8,128)(2,1)} copy(bf16[3456,256]{0,1:T(8,128)(2,1)S(1)} %bitcast.124) | data formatting | bytes 3538944 | tf_op jit(solution)/shard_map/dot_general | solution.py:105
  48.2 2.0 %multiply_reduce_fusion.2 = (f32[256]{0:T(256)S(1)}, f32[256,128]{1,0:T(8,128)S(1)}) fusion(bf16[256,3456]{1,0:T(8,128)(2,1)S(1)} %constant_dynamic-update-slice_fusion.27, bf16[3456,128]{1,0:T(8,128)(2,1)} %bitcast.130), kind=kOutput, calls=%fused_computation.162 | convolution fusion | flops 226557696 | bytes 2786304 | tf_op jit(solution)/shard_map/dot_general | solution.py:83
  50.7 1.3 collective-permute-start.6
  52.6 4.2 %collective-permute-done.6 = bf16[2,4,32,128]{3,2,1,0:T(8,128)(2,1)S(1)} collective-permute-done((bf16[2,4,32,128]{3,2,1,0:T(8,128)(2,1)S(1)}, bf16[2,4,32,128]{3,2,1,0:T(8,128)(2,1)S(1)}, u32[]{:S(2)}, u32[]{:S(2)}) %collective-permute-start.6) | collective-permute-done | bytes 65568 | tf_op jit(solution)/shard_map/ppermute | solution.py:14
  56.9 3.2 %collective-permute-start.7 = (bf16[4,1,32,128]{3,2,1,0:T(8,128)(2,1)S(1)}, bf16[4,1,32,128]{3,2,1,0:T(8,128)(2,1)S(1)}, u32[]{:S(2)}, u32[]{:S(2)}) collective-permute-start(bf16[4,1,32,128]{3,2,1,0:T(8,128)(2,1)S(1)} %get-tuple-element.92), channel_id=1, source_target_pairs={{0,1},{1,2},{2,3},{3,4},{4,5},{5,6},{6,7},{8,9},{9,10},{10,11},{11... | collective-permute-start | bytes 98312 | tf_op jit(solution)/shard_map/ppermute | solution.py:25
  60.0 1.3 collective-permute-start.8
  61.4 2.4 %collective-permute-done.8 = bf16[4,1,32,128]{3,2,1,0:T(8,128)(2,1)S(1)} collective-permute-done((bf16[4,1,32,128]{3,2,1,0:T(8,128)(2,1)S(1)}, bf16[4,1,32,128]{3,2,1,0:T(8,128)(2,1)S(1)}, u32[]{:S(2)}, u32[]{:S(2)}) %collective-permute-start.8) | collective-permute-done | bytes 32800 | tf_op jit(solution)/shard_map/ppermute | solution.py:27
  65.5 0.7 multiply_reduce_fusion
  67.0 1.3 collective-permute-start.9
  68.3 1.4 pad_maximum_fusion
  69.7 3.6 %collective-permute-done.9 = bf16[2,4,32,128]{3,2,1,0:T(8,128)(2,1)S(1)} collective-permute-done((bf16[2,4,32,128]{3,2,1,0:T(8,128)(2,1)S(1)}, bf16[2,4,32,128]{3,2,1,0:T(8,128)(2,1)S(1)}, u32[]{:S(2)}, u32[]{:S(2)}) %collective-permute-start.9) | collective-permute-done | bytes 65568 | tf_op jit(solution)/shard_map/ppermute | solution.py:14
  73.3 3.7 %collective-permute-start.10 = (bf16[4,1,32,128]{3,2,1,0:T(8,128)(2,1)S(1)}, bf16[4,1,32,128]{3,2,1,0:T(8,128)(2,1)S(1)}, u32[]{:S(2)}, u32[]{:S(2)}) collective-permute-start(bf16[4,1,32,128]{3,2,1,0:T(8,128)(2,1)S(1)} %get-tuple-element.88), channel_id=1, source_target_pairs={{0,1},{1,2},{2,3},{3,4},{4,5},{5,6},{6,7},{8,9},{9,10},{10,11},{11... | collective-permute-start | bytes 98312 | tf_op jit(solution)/shard_map/ppermute | solution.py:25
  77.0 1.3 collective-permute-start.11
  78.3 2.2 %collective-permute-done.11 = bf16[4,1,32,128]{3,2,1,0:T(8,128)(2,1)S(1)} collective-permute-done((bf16[4,1,32,128]{3,2,1,0:T(8,128)(2,1)S(1)}, bf16[4,1,32,128]{3,2,1,0:T(8,128)(2,1)S(1)}, u32[]{:S(2)}, u32[]{:S(2)}) %collective-permute-start.11) | collective-permute-done | bytes 32800 | tf_op jit(solution)/shard_map/ppermute | solution.py:27
  80.8 0.6 constant_dynamic-update-slice_fusion.107
  81.5 0.7 constant_dynamic-update-slice_fusion.106
  82.1 0.6 constant_dynamic-update-slice_fusion.105
  82.8 0.6 constant_dynamic-update-slice_fusion.104
  83.4 0.6 constant_dynamic-update-slice_fusion.103
  84.1 0.7 constant_dynamic-update-slice_fusion.102
  84.7 0.7 constant_dynamic-update-slice_fusion.101
  85.4 0.7 constant_dynamic-update-slice_fusion.100
  86.1 0.6 constant_dynamic-update-slice_fusion.99
  87.4 0.7 constant_dynamic-update-slice_fusion.97
  88.1 0.7 constant_dynamic-update-slice_fusion.96
  88.7 0.7 constant_dynamic-update-slice_fusion.95
  89.4 0.6 constant_dynamic-update-slice_fusion.94
  91.3 0.6 constant_dynamic-update-slice_fusion.91
  91.9 0.7 constant_dynamic-update-slice_fusion.90
  93.2 0.7 constant_dynamic-update-slice_fusion.88
  93.8 0.6 constant_dynamic-update-slice_fusion.87
  94.5 0.7 constant_dynamic-update-slice_fusion.86
  95.2 0.6 constant_dynamic-update-slice_fusion.85
  95.8 0.6 constant_dynamic-update-slice_fusion.84
  96.4 0.7 constant_dynamic-update-slice_fusion.83
  97.1 12.3 %reduce-scatter.3.cloned.1.call-done = bf16[54,16,128]{2,1,0:T(8,128)(2,1)} async-done(((bf16[54,128,128]{2,1,0:T(8,128)(2,1)}), bf16[54,16,128]{2,1,0:T(8,128)(2,1)}) %reduce-scatter.3.cloned.1.call-update) | async-done | bytes 221200 | tf_op jit(solution)/shard_map/reduce_scatter | solution.py:117
  109.4 2.2 %copy.24 = bf16[54,16,128]{0,1,2:T(8,128)(2,1)} copy(bf16[54,16,128]{2,1,0:T(8,128)(2,1)} %reduce-scatter.3.cloned.1.call-done) | data formatting | bytes 442368 | tf_op jit(solution)/shard_map/reduce_scatter | solution.py:117
  111.7 0.7 constant_dynamic-update-slice_fusion.82
  112.3 0.7 constant_dynamic-update-slice_fusion.81
  113.0 2.7 %convolution_convert_fusion.2 = bf16[256,128]{1,0:T(8,128)(2,1)} fusion(bf16[256,3456]{1,0:T(8,128)(2,1)} %constant_dynamic-update-slice_fusion.81, bf16[3456,128]{1,0:T(8,128)(2,1)S(1)} %bitcast.129), kind=kOutput, calls=%fused_computation.3 | convolution fusion | flops 226525184 | bytes 2719744 | tf_op jit(solution)/shard_map/dot_general | solution.py:112
  115.7 19.3 %reduce-scatter.5.cloned.1.call-done = bf16[54,16,32]{0,1,2:T(8,128)(2,1)} async-done(((bf16[54,16,128]{0,1,2:T(8,128)(2,1)}), bf16[54,16,32]{0,1,2:T(8,128)(2,1)}) %reduce-scatter.5.cloned.1.call-update) | async-done | bytes 55312 | tf_op jit(solution)/shard_map/reduce_scatter | solution.py:120
  135.0 0.9 convert_multiply_fusion
  135.9 0.8 copy.25
  (142 shorter events, 8.2 us)
Async XLA Ops:
  7.2 102.2 %reduce-scatter.3.cloned.1.call-start = ((), (), s32[]{:S(2)}) async-start(), calls=%async_computation.2 | async-start | bytes 1990656 | tf_op jit(solution)/shard_map/reduce_scatter | solution.py:117
  8.2 10.9 %copy-start.9 = (f32[2,128]{1,0:T(2,128)S(1)}, f32[2,128]{1,0:T(2,128)}, u32[]{:S(2)}) copy-start(f32[2,128]{1,0:T(2,128)} %param.8) | copy-start | bytes 3076
  8.2 8.1 %collective-permute-start = (bf16[2,4,32,128]{3,2,1,0:T(8,128)(2,1)S(1)}, bf16[2,4,32,128]{3,2,1,0:T(8,128)(2,1)S(1)}, u32[]{:S(2)}, u32[]{:S(2)}) collective-permute-start(bf16[2,4,32,128]{3,2,1,0:T(8,128)(2,1)S(1)} %multiply_convert_fusion.1), channel_id=1, source_target_pairs={{0,8},{8,16},{16,24},{1,9},{9,17},{17,25},{2,10},{10,18},{18,26},{... | collective-permute-start | bytes 196616 | tf_op jit(solution)/shard_map/ppermute | solution.py:14
  16.3 2.8 %collective-permute-start.1 = (bf16[4,1,32,128]{3,2,1,0:T(8,128)(2,1)S(1)}, bf16[4,1,32,128]{3,2,1,0:T(8,128)(2,1)S(1)}, u32[]{:S(2)}, u32[]{:S(2)}) collective-permute-start(bf16[4,1,32,128]{3,2,1,0:T(8,128)(2,1)S(1)} %get-tuple-element.100), channel_id=1, source_target_pairs={{0,1},{1,2},{2,3},{3,4},{4,5},{5,6},{6,7},{8,9},{9,10},{10,11},{11... | collective-permute-start | bytes 98312 | tf_op jit(solution)/shard_map/ppermute | solution.py:25
  17.8 4.7 %collective-permute-start.2 = (bf16[4,1,32,128]{3,2,1,0:T(8,128)(2,1)S(1)}, bf16[4,1,32,128]{3,2,1,0:T(8,128)(2,1)S(1)}, u32[]{:S(2)}, u32[]{:S(2)}) collective-permute-start(bf16[4,1,32,128]{3,2,1,0:T(8,128)(2,1)S(1)} %get-tuple-element.101), channel_id=1, source_target_pairs={{1,0},{2,1},{3,2},{4,3},{5,4},{6,5},{7,6},{9,8},{10,9},{11,10},{12... | collective-permute-start | bytes 98312 | tf_op jit(solution)/shard_map/ppermute | solution.py:27
  22.6 0.8 copy-start.6
  22.6 0.8 copy-start.8
  24.4 0.7 copy-start.2
  25.8 8.2 %collective-permute-start.3 = (bf16[2,4,32,128]{3,2,1,0:T(8,128)(2,1)}, bf16[2,4,32,128]{3,2,1,0:T(8,128)(2,1)}, u32[]{:S(2)}, u32[]{:S(2)}) collective-permute-start(bf16[2,4,32,128]{3,2,1,0:T(8,128)(2,1)} %bitcast.3), channel_id=1, source_target_pairs={{0,8},{8,16},{16,24},{1,9},{9,17},{17,25},{2,10},{10,18},{18,26},{... | collective-permute-start | bytes 196616 | tf_op jit(solution)/shard_map/ppermute | solution.py:14
  34.8 6.3 %collective-permute-start.4 = (bf16[4,1,32,128]{3,2,1,0:T(8,128)(2,1)S(1)}, bf16[4,1,32,128]{3,2,1,0:T(8,128)(2,1)S(1)}, u32[]{:S(2)}, u32[]{:S(2)}) collective-permute-start(bf16[4,1,32,128]{3,2,1,0:T(8,128)(2,1)S(1)} %get-tuple-element.96), channel_id=1, source_target_pairs={{0,1},{1,2},{2,3},{3,4},{4,5},{5,6},{6,7},{8,9},{9,10},{10,11},{11... | collective-permute-start | bytes 98312 | tf_op jit(solution)/shard_map/ppermute | solution.py:25
  39.0 3.1 %collective-permute-start.5 = (bf16[4,1,32,128]{3,2,1,0:T(8,128)(2,1)S(1)}, bf16[4,1,32,128]{3,2,1,0:T(8,128)(2,1)S(1)}, u32[]{:S(2)}, u32[]{:S(2)}) collective-permute-start(bf16[4,1,32,128]{3,2,1,0:T(8,128)(2,1)S(1)} %get-tuple-element.97), channel_id=1, source_target_pairs={{1,0},{2,1},{3,2},{4,3},{5,4},{6,5},{7,6},{9,8},{10,9},{11,10},{12... | collective-permute-start | bytes 98312 | tf_op jit(solution)/shard_map/ppermute | solution.py:27
  44.3 1.5 %copy-start.3 = (f32[256,128]{1,0:T(8,128)S(1)}, f32[256,128]{1,0:T(8,128)}, u32[]{:S(2)}) copy-start(f32[256,128]{1,0:T(8,128)} %copy-done.2) | copy-start | bytes 393220
  48.2 2.0 %copy-start.7 = (bf16[2,4,32,128]{3,2,1,0:T(8,128)(2,1)S(1)}, bf16[2,4,32,128]{3,2,1,0:T(8,128)(2,1)}, u32[]{:S(2)}) copy-start(bf16[2,4,32,128]{3,2,1,0:T(8,128)(2,1)} %param.9) | copy-start | bytes 196612
  48.2 3.8 %copy-start = (bf16[3456,256]{1,0:T(8,128)(2,1)S(1)}, bf16[3456,256]{1,0:T(8,128)(2,1)}, u32[]{:S(2)}) copy-start(bf16[3456,256]{1,0:T(8,128)(2,1)} %copy.23) | copy-start | bytes 5308420
  50.7 6.2 %collective-permute-start.6 = (bf16[2,4,32,128]{3,2,1,0:T(8,128)(2,1)S(1)}, bf16[2,4,32,128]{3,2,1,0:T(8,128)(2,1)S(1)}, u32[]{:S(2)}, u32[]{:S(2)}) collective-permute-start(bf16[2,4,32,128]{3,2,1,0:T(8,128)(2,1)S(1)} %bitcast.137), channel_id=1, source_target_pairs={{8,0},{16,8},{24,16},{9,1},{17,9},{25,17},{10,2},{18,10},{26,18},{... | collective-permute-start | bytes 196616 | tf_op jit(solution)/shard_map/ppermute | solution.py:14
  56.9 4.5 %collective-permute-start.7 = (bf16[4,1,32,128]{3,2,1,0:T(8,128)(2,1)S(1)}, bf16[4,1,32,128]{3,2,1,0:T(8,128)(2,1)S(1)}, u32[]{:S(2)}, u32[]{:S(2)}) collective-permute-start(bf16[4,1,32,128]{3,2,1,0:T(8,128)(2,1)S(1)} %get-tuple-element.92), channel_id=1, source_target_pairs={{0,1},{1,2},{2,3},{3,4},{4,5},{5,6},{6,7},{8,9},{9,10},{10,11},{11... | collective-permute-start | bytes 98312 | tf_op jit(solution)/shard_map/ppermute | solution.py:25
  60.0 3.8 %collective-permute-start.8 = (bf16[4,1,32,128]{3,2,1,0:T(8,128)(2,1)S(1)}, bf16[4,1,32,128]{3,2,1,0:T(8,128)(2,1)S(1)}, u32[]{:S(2)}, u32[]{:S(2)}) collective-permute-start(bf16[4,1,32,128]{3,2,1,0:T(8,128)(2,1)S(1)} %get-tuple-element.93), channel_id=1, source_target_pairs={{1,0},{2,1},{3,2},{4,3},{5,4},{6,5},{7,6},{9,8},{10,9},{11,10},{12... | collective-permute-start | bytes 98312 | tf_op jit(solution)/shard_map/ppermute | solution.py:27
  64.2 0.9 copy-start.4
  64.2 1.2 copy-start.5
  67.0 6.4 %collective-permute-start.9 = (bf16[2,4,32,128]{3,2,1,0:T(8,128)(2,1)S(1)}, bf16[2,4,32,128]{3,2,1,0:T(8,128)(2,1)S(1)}, u32[]{:S(2)}, u32[]{:S(2)}) collective-permute-start(bf16[2,4,32,128]{3,2,1,0:T(8,128)(2,1)S(1)} %bitcast.132), channel_id=1, source_target_pairs={{8,0},{16,8},{24,16},{9,1},{17,9},{25,17},{10,2},{18,10},{26,18},{... | collective-permute-start | bytes 196616 | tf_op jit(solution)/shard_map/ppermute | solution.py:14
  69.7 65.3 %reduce-scatter.5.cloned.1.call-start = ((), (), s32[]{:S(2)}) async-start(), calls=%async_computation.3 | async-start | bytes 655360 | tf_op jit(solution)/shard_map/reduce_scatter | solution.py:120
  73.3 5.0 %collective-permute-start.10 = (bf16[4,1,32,128]{3,2,1,0:T(8,128)(2,1)S(1)}, bf16[4,1,32,128]{3,2,1,0:T(8,128)(2,1)S(1)}, u32[]{:S(2)}, u32[]{:S(2)}) collective-permute-start(bf16[4,1,32,128]{3,2,1,0:T(8,128)(2,1)S(1)} %get-tuple-element.88), channel_id=1, source_target_pairs={{0,1},{1,2},{2,3},{3,4},{4,5},{5,6},{6,7},{8,9},{9,10},{10,11},{11... | collective-permute-start | bytes 98312 | tf_op jit(solution)/shard_map/ppermute | solution.py:25
  77.0 3.5 %collective-permute-start.11 = (bf16[4,1,32,128]{3,2,1,0:T(8,128)(2,1)S(1)}, bf16[4,1,32,128]{3,2,1,0:T(8,128)(2,1)S(1)}, u32[]{:S(2)}, u32[]{:S(2)}) collective-permute-start(bf16[4,1,32,128]{3,2,1,0:T(8,128)(2,1)S(1)} %get-tuple-element.89), channel_id=1, source_target_pairs={{1,0},{2,1},{3,2},{4,3},{5,4},{6,5},{7,6},{9,8},{10,9},{11,10},{12... | collective-permute-start | bytes 98312 | tf_op jit(solution)/shard_map/ppermute | solution.py:27
  87.4 25.6 %copy-start.1 = (bf16[27,128,128]{2,1,0:T(8,128)(2,1)S(1)}, bf16[27,128,128]{2,1,0:T(8,128)(2,1)}, u32[]{:S(2)}) copy-start(bf16[27,128,128]{2,1,0:T(8,128)(2,1)} %copy.21) | copy-start | bytes 2654212
Sparse Core Ops, SparseCore 0:
  69.8 39.5 reduce-scatter.2
  112.2 22.7 reduce-scatter.4
where the time goes:
time: 144 us
  waiting for transfers between devices  48.5 us (34%)
  local copies, waits for them, and re-layouts  34.7 us (24%)
  starting transfers between devices  29.3 us (20%)
  between operations  14.9 us (10%)
  other arithmetic  8.77 us (6%)
  matrix products  7.39 us (5%)
    unnamed x122, local copies, waits for them, and re-layouts  21.5 us
    reduce_scatter x1, waiting for transfers between devices, local(): lax.psum_scatter(partial_sum, 'frame', scatter_dimension=2, tiled=True)  19.3 us
    ppermute x4, starting transfers between devices, with_halo(): lax.ppermute(tail, axis, [(i, (i + 1) % count) for i in range(ends)])  12.5 us
    reduce_scatter x1, waiting for transfers between devices, local(): lax.psum_scatter(stacked.astype(jnp.bfloat16), 'tile', scatter_dimension=...  12.3 us
    ppermute x4, starting transfers between devices, from_behind(): lax.ppermute(value, axis, [(source, source + steps) for source in range(f...  11.5 us
    ppermute x4, waiting for transfers between devices, with_halo(): lax.ppermute(head, axis, [((i + 1) % count, i) for i in range(ends)])  9 us
    ppermute x4, waiting for transfers between devices, from_behind(): lax.ppermute(value, axis, [(source, source + steps) for source in range(f...  7.84 us
    transpose x3, local copies, waits for them, and re-layouts, local(): jnp.transpose(kernels[layer], (0, 2, 1)).reshape(27 * channels, channels)  6.48 us
  transfers between devices with their start and end apart: 14, of which 8 were waited for; matrix products, arithmetic and copies ran while one was open for 21% of the time, Pallas kernels for 0%

commit v1 on v0

v1 whole, which is shorter than its diff:
```python
import functools
import math

import jax
import jax.numpy as jnp
from jax import lax
from jax.experimental import pallas as pl
from jax.experimental.pallas import tpu as pltpu
from jax.sharding import PartitionSpec as P

EPS = 1e-06
MESH = pl.DeviceIdType.MESH
F32 = jnp.float32
BF16 = jnp.bfloat16


def sigmoid(value):
    return 1.0 / (1.0 + jnp.exp(-value))


def kernel(
    sizes,
    x_in,
    w_in,
    gains_ref,
    cot_in,
    grad_ref,
    kg_ref,
    ext,
    weights,
    turned,
    cot,
    patch,
    patch_back,
    z_keep,
    pair_out,
    pair_in,
    ring_out,
    ring_in,
    total,
    pack_out,
    pack_in,
    local_sem,
    halo_send,
    halo_recv,
    pair_send,
    pair_recv,
    ring_send,
    ring_recv,
    pack_send,
    pack_recv,
):
    nf, nt, layers, frames, rows, columns, channels = sizes
    f = lax.axis_index("frame")
    t = lax.axis_index("tile")
    pairs = nt // 2
    core = t % 2
    place = t // 2
    block = rows * columns
    cells = frames * block
    own_q = channels // nt
    own_o = channels // nf
    group = -(-27 // nf)

    x_copy = pltpu.make_async_copy(
        x_in, ext.at[0, frames : 2 * frames, 1 : 1 + rows], local_sem.at[0]
    )
    w_copies = [
        pltpu.make_async_copy(w_in.at[l], weights.at[l], local_sem.at[1 + l]) for l in range(layers)
    ]
    cot_copy = pltpu.make_async_copy(cot_in, cot, local_sem.at[1 + layers])
    for e in range(2 * layers):
        edge = jnp.zeros((2 * frames, 1, columns, channels), BF16)
        ext[e, :, 0:1] = edge
        ext[e, :, rows + 1 : rows + 2] = edge
        far = 0 if e < layers else frames
        ext[e, far : far + frames, 1 : 1 + rows] = jnp.zeros(
            (frames, rows, columns, channels), BF16
        )
    x_copy.start()
    for c in w_copies:
        c.start()
    cot_copy.start()

    offsets = {(0, 1), (0, nt - 1)}
    for df in (1, nf - 1):
        for dt in (0, 1, nt - 1):
            offsets.add((df, dt))
    for s in range(1, pairs):
        offsets.add((0, 2 * s))
    for s in range(1, nf):
        offsets.add((s, 0))
    offsets = sorted(offsets)
    barrier = pltpu.get_barrier_semaphore()
    for df, dt in offsets:
        pl.semaphore_signal(
            barrier,
            inc=1,
            device_id=((f + df) % nf, (t + dt) % nt),
            device_id_type=MESH,
        )
    pl.semaphore_wait(barrier, len(offsets))

    def halo(e):
        step = 1 if e < layers else -1
        own = frames if step > 0 else 0
        far = 0 if step > 0 else frames
        messages = []
        for index, (df, dt) in enumerate(((step, 0), (0, 1), (0, -1), (step, 1), (step, -1))):
            if dt == 0:
                src_rows, dst_rows = (1, 1 + rows), (1, 1 + rows)
            elif dt > 0:
                src_rows, dst_rows = (rows, rows + 1), (0, 1)
            else:
                src_rows, dst_rows = (1, 2), (rows + 1, rows + 2)
            start = far if df else own
            to_f, to_t, from_f, from_t = f + df, t + dt, f - df, t - dt
            can_send = (to_f >= 0) & (to_f < nf) & (to_t >= 0) & (to_t < nt)
            can_recv = (from_f >= 0) & (from_f < nf) & (from_t >= 0) & (from_t < nt)
            copy = pltpu.make_async_remote_copy(
                src_ref=ext.at[e, own : own + frames, src_rows[0] : src_rows[1]],
                dst_ref=ext.at[e, start : start + frames, dst_rows[0] : dst_rows[1]],
                send_sem=halo_send.at[e, index],
                recv_sem=halo_recv.at[e, index],
                device_id=((f + df) % nf, (t + dt) % nt),
                device_id_type=MESH,
            )
            messages.append((copy, can_send, can_recv))
        return messages

    halos = [halo(e) for e in range(2 * layers)]

    def send_halo(e):
        for copy, can_send, _ in halos[e]:
            pl.when(can_send)(copy.start)

    def wait_halo(e):
        for copy, _, can_recv in halos[e]:
            pl.when(can_recv)(copy.wait_recv)

    height = 2 * frames * (rows + 2) * columns
    column = lax.broadcasted_iota(jnp.int32, (height, channels), 0) % columns

    def fill(target, e):
        flat = ext[e].astype(F32).reshape(height, channels)
        before = jnp.where(column == 0, 0.0, pltpu.roll(flat, 1, 0)).astype(BF16)
        after = jnp.where(column == columns - 1, 0.0, pltpu.roll(flat, height - 1, 0)).astype(BF16)
        for c, value in enumerate((before, ext[e].reshape(height, channels), after)):
            value = value.reshape(2 * frames, rows + 2, columns, channels)
            for b in range(3):
                at = (3 * b + c) * channels
                target[:, at : at + channels] = value[:, b : b + rows].reshape(
                    2 * cells, channels
                )

    def turn(l):
        for k in range(27):
            a, m = k // 9, 8 - k % 9
            turned[l, a, m * channels : (m + 1) * channels, :] = weights[l, k].T

    def pair_copy(l, a):
        return pltpu.make_async_remote_copy(
            src_ref=pair_out.at[l, a, 1 - core],
            dst_ref=pair_in.at[l, a],
            send_sem=pair_send.at[l, a],
            recv_sem=pair_recv.at[l, a],
            device_id=(f, t + 1 - 2 * core),
            device_id_type=MESH,
        )

    def ring_copy(l, a, s):
        peer = (place + s) % pairs
        return pltpu.make_async_remote_copy(
            src_ref=ring_out.at[l, a, peer],
            dst_ref=ring_in.at[l, a, s - 1],
            send_sem=ring_send.at[l, a, s - 1],
            recv_sem=ring_recv.at[l, a, s - 1],
            device_id=(f, 2 * peer + core),
            device_id_type=MESH,
        )

    def pack_copy(l, s):
        peer = (f + s) % nf
        return pltpu.make_async_remote_copy(
            src_ref=pack_out.at[l, peer],
            dst_ref=pack_in.at[l, s - 1],
            send_sem=pack_send.at[l, s - 1],
            recv_sem=pack_recv.at[l, s - 1],
            device_id=(peer, t),
            device_id_type=MESH,
        )

    def kernel_terms(l, pre_grad):
        for a in range(3):
            part = lax.dot_general(
                patch[l, a * block : a * block + cells, :],
                pre_grad,
                (((0,), (0,)), ((), ())),
                preferred_element_type=F32,
            )
            part = part.astype(BF16).reshape(9, channels, channels)
            for d in range(nt):
                pair_out[l, a, d % 2, d // 2] = part[:, d * own_q : (d + 1) * own_q]
            pair_copy(l, a).start()

    def ring_stage(l):
        for a in range(3):
            pair_copy(l, a).wait_recv()
            for s in range(1, pairs):
                peer = (place + s) % pairs
                ring_out[l, a, peer] = (
                    pair_out[l, a, core, peer].astype(F32) + pair_in[l, a, peer].astype(F32)
                ).astype(BF16)
                ring_copy(l, a, s).start()
            total[l, 9 * a : 9 * a + 9] = pair_out[l, a, core, place].astype(F32) + pair_in[
                l, a, place
            ].astype(F32)

    lane_block = lax.broadcasted_iota(jnp.int32, (group, own_q, channels), 2) // own_o

    def pack_stage(l):
        for a in range(3):
            value = total[l, 9 * a : 9 * a + 9]
            for s in range(1, pairs):
                ring_copy(l, a, s).wait_recv()
                value = value + ring_in[l, a, s - 1].astype(F32)
            total[l, 9 * a : 9 * a + 9] = value
        for d in range(nf):
            packed = jnp.zeros((group, own_q, channels), F32)
            for j in range(nf):
                piece = total[l, j * group : (j + 1) * group]
                shift = ((j - d) * own_o) % channels
                if shift:
                    piece = pltpu.roll(
                        piece.reshape(group * own_q, channels), shift, 1
                    ).reshape(group, own_q, channels)
                packed = jnp.where(lane_block == j, piece, packed)
            pack_out[l, d] = packed.astype(BF16)
        for s in range(1, nf):
            pack_copy(l, s).start()

    def finish(l):
        value = pack_out[l, f].astype(F32)
        for s in range(1, nf):
            pack_copy(l, s).wait_recv()
            value = value + pack_in[l, s - 1].astype(F32)
        for j in range(nf):
            low, high = j * group, min(27, (j + 1) * group)
            if low >= high:
                break
            moved = value
            if j:
                moved = pltpu.roll(
                    value.reshape(group * own_q, channels), channels - j * own_o, 1
                ).reshape(group, own_q, channels)
            kg_ref[27 * l + low : 27 * l + high] = moved[: high - low, :, :own_o]

    x_copy.wait()
    send_halo(0)
    for l in range(layers):
        total[l, 27:] = jnp.zeros((nf * group - 27, own_q, channels), F32)
    for l in range(layers):
        w_copies[l].wait()
        if l == 0:
            turn(layers - 1 if layers == 1 else 0)
        else:
            turn(l)
        wait_halo(l)
        fill(patch.at[l], l)
        z = jnp.zeros((cells, channels), F32)
        for a in range(3):
            z = z + jnp.dot(
                patch[l, a * block : a * block + cells, :],
                weights[l, 9 * a : 9 * a + 9].reshape(9 * channels, channels),
                preferred_element_type=F32,
            )
        z_keep[l] = z
        if l + 1 < layers:
            inverse = lax.rsqrt(jnp.mean(z * z, axis=-1, keepdims=True) + EPS)
            normed = z * inverse * gains_ref[l : l + 1, :]
            ext[l + 1, frames : 2 * frames, 1 : 1 + rows] = (
                (normed * sigmoid(normed)).astype(BF16).reshape(frames, rows, columns, channels)
            )
            send_halo(l + 1)

    cot_copy.wait()
    upstream = cot[...].astype(F32).reshape(cells, channels)
    for l in reversed(range(layers)):
        e = layers + l
        z = z_keep[l]
        gain = gains_ref[l : l + 1, :]
        inverse = lax.rsqrt(jnp.mean(z * z, axis=-1, keepdims=True) + EPS)
        normed = z * inverse * gain
        sigma = sigmoid(normed)
        scaled = gain * upstream * sigma * (1.0 + normed * (1.0 - sigma))
        mixed = jnp.mean(z * scaled, axis=-1, keepdims=True)
        pre_grad = (inverse * scaled - z * (inverse * inverse * inverse * mixed)).astype(BF16)
        ext[e, 0:frames, 1 : 1 + rows] = pre_grad.reshape(frames, rows, columns, channels)
        send_halo(e)
        kernel_terms(l, pre_grad)
        if l + 1 < layers:
            pack_stage(l + 1)
        ring_stage(l)
        wait_halo(e)
        fill(patch_back, e)
        back = jnp.zeros((cells, channels), F32)
        for a in range(3):
            start = (2 - a) * block
            back = back + jnp.dot(
                patch_back[start : start + cells, :], turned[l, a], preferred_element_type=F32
            )
        back = back.astype(BF16)
        upstream = back.astype(F32)
        if l + 1 < layers:
            finish(l + 1)
    grad_ref[...] = back.reshape(frames, rows, columns, channels)
    pack_stage(0)
    finish(0)

    for e in range(2 * layers):
        for copy, can_send, _ in halos[e]:
            pl.when(can_send)(copy.wait_send)
    for l in range(layers):
        for a in range(3):
            pair_copy(l, a).wait_send()
            for s in range(1, pairs):
                ring_copy(l, a, s).wait_send()
        for s in range(1, nf):
            pack_copy(l, s).wait_send()


def local(saved_codes, saved_scales, kernels, norm_gains, cotangent):
    nf, nt = lax.axis_size("frame"), lax.axis_size("tile")
    frames, rows, columns, channels = saved_codes.shape
    layers = kernels.shape[0]
    assert frames == 2
    block = rows * columns
    cells = frames * block
    pairs = nt // 2
    own_q, own_o = channels // nt, channels // nf
    group = -(-27 // nf)
    layer_in = (saved_codes.astype(F32) * saved_scales[..., None]).astype(BF16)
    vmem = pl.BlockSpec(memory_space=pltpu.VMEM)
    anywhere = pl.BlockSpec(memory_space=pl.ANY)
    dma = pltpu.SemaphoreType.DMA
    input_grad, summed = pl.pallas_call(
        functools.partial(kernel, (nf, nt, layers, frames, rows, columns, channels)),
        out_shape=(
            jax.ShapeDtypeStruct((frames, rows, columns, channels), BF16),
            jax.ShapeDtypeStruct((27 * layers, own_q, own_o), F32),
        ),
        in_specs=[anywhere, anywhere, vmem, anywhere],
        out_specs=(vmem, vmem),
        scratch_shapes=[
            pltpu.VMEM((2 * layers, 2 * frames, rows + 2, columns, channels), BF16),
            pltpu.VMEM((layers, 27, channels, channels), BF16),
            pltpu.VMEM((layers, 3, 9 * channels, channels), BF16),
            pltpu.VMEM((frames, rows, columns, channels), BF16),
            pltpu.VMEM((layers, 2 * cells, 9 * channels), BF16),
            pltpu.VMEM((2 * cells, 9 * channels), BF16),
            pltpu.VMEM((layers, cells, channels), F32),
            pltpu.VMEM((layers, 3, 2, pairs, 9, own_q, channels), BF16),
            pltpu.VMEM((layers, 3, pairs, 9, own_q, channels), BF16),
            pltpu.VMEM((layers, 3, pairs, 9, own_q, channels), BF16),
            pltpu.VMEM((layers, 3, pairs - 1, 9, own_q, channels), BF16),
            pltpu.VMEM((layers, nf * group, own_q, channels), F32),
            pltpu.VMEM((layers, nf, group, own_q, channels), BF16),
            pltpu.VMEM((layers, nf - 1, group, own_q, channels), BF16),
            dma((2 + layers,)),
            dma((2 * layers, 5)),
            dma((2 * layers, 5)),
            dma((layers, 3)),
            dma((layers, 3)),
            dma((layers, 3, pairs - 1)),
            dma((layers, 3, pairs - 1)),
            dma((layers, nf - 1)),
            dma((layers, nf - 1)),
        ],
        compiler_params=pltpu.CompilerParams(
            collective_id=0, has_side_effects=True, vmem_limit_bytes=50 * 1024 * 1024
        ),
    )(layer_in, kernels, norm_gains, cotangent)
    total_cells = cells * nf * nt
    return input_grad, summed / jnp.float32(math.sqrt(total_cells))


def solution(mesh):
    in_specs = (
        P("frame", "tile", None, None),
        P("frame", "tile", None),
        P(),
        P(),
        P("frame", "tile", None, None),
    )
    out_specs = (P("frame", "tile", None, None), P(None, "tile", "frame"))
    return jax.shard_map(local, mesh=mesh, in_specs=in_specs, out_specs=out_specs, check_vma=False)
```

time: 144 us -> 50.6 us (0.35)
  waiting for transfers between devices: 48.5 us -> 0 us
  Pallas kernels: 0 us -> 44.1 us
  local copies, waits for them, and re-layouts: 34.7 us -> 4.57 us
  starting transfers between devices: 29.3 us -> 0 us
  between operations: 14.9 us -> 0.66 us
  other arithmetic: 8.77 us -> 0.98 us
  matrix products: 7.39 us -> 0 us
    pallas_call x0 -> x1, Pallas kernels: none -> 44.1 us  [local(): pl.pallas_call(functools.partial(kernel, (nf, nt, layers, frames, rows, c...]
    reduce_scatter x2 -> x0, waiting for transfers between devices: 31.6 us -> none  [the longest x1 19.3 us: local(): lax.psum_scatter(partial_sum, 'frame', scatter_dimension=2, tiled=True)]
    ppermute x12 -> x0, starting transfers between devices: 29.2 us -> none  [the longest x4 12.5 us: with_halo(): lax.ppermute(tail, axis, [(i, (i + 1) % count) for i in range(ends)])]
    unnamed x122 -> x8, local copies, waits for them, and re-layouts: 21.5 us -> 4.57 us
    ppermute x12 -> x0, waiting for transfers between devices: 16.9 us -> none  [the longest x4 9 us: with_halo(): lax.ppermute(head, axis, [((i + 1) % count, i) for i in range(ends)])]
    dot_general x6 -> x0, matrix products: 7.39 us -> none  [the longest x2 3.44 us: local(): jnp.dot(columns_back, back_kernel, preferred_element_type=jnp.float32)]
    transpose x3 -> x0, local copies, waits for them, and re-layouts: 6.48 us -> none  [local(): jnp.transpose(kernels[layer], (0, 2, 1)).reshape(27 * channels, channels)]
    concatenate x12 -> x0, other arithmetic: 4.48 us -> none  [the longest x8 2.29 us: with_halo(): jnp.concatenate([lax.ppermute(tail, axis, [(i, (i + 1) % count) for i in...]
  transfers between devices with their start and end apart: 14 -> 0, of which waited for: 8 -> 0; matrix products, arithmetic and copies ran while one was open for 21% -> 0% of each run, Pallas kernels for 0% -> 0%
where the time goes in v1:
time: 50.6 us; the launch traced here: 50.3 us
  Pallas kernels  44.1 us (87%)
  local copies, waits for them, and re-layouts  4.57 us (9%)
  other arithmetic  0.98 us (2%)
  between operations  0.66 us (1%)
    pallas_call x1, Pallas kernels, local(): pl.pallas_call(functools.partial(kernel, (nf, nt, layers, frames, rows, c...  44.1 us
    unnamed x8, local copies, waits for them, and re-layouts  4.57 us

profile of v1, /device:TPU:0, one launch (start us, length us, event | category | flops | bytes accessed | tf_op | source)
XLA Modules:
  0.0 50.3 jit_solution(477872005868269219)
XLA Ops:
  0.6 0.9 %multiply_convert_fusion.x_in = bf16[2,4,32,128]{3,2,1,0:T(8,128)(2,1)S(1)} fusion(bf16[2,4,32,128]{3,2,1,0:T(8,128)(2,1)} %param.5, f32[2,4,32]{2,1,0:T(4,128)} %param.6), kind=kLoop, calls=%fused_computation.1 | loop fusion | flops 98304 | bytes 132096 | tf_op jit(solution)/shard_map/convert_element_type | solution.py:342
  1.6 0.0 copy-start
  1.6 1.5 %copy-done = bf16[2,27,128,128]{3,2,1,0:T(8,128)(2,1)S(1)} copy-done((bf16[2,27,128,128]{3,2,1,0:T(8,128)(2,1)S(1)}, bf16[2,27,128,128]{3,2,1,0:T(8,128)(2,1)}, u32[]{:S(2)}) %copy-start) | copy-done | bytes 1769496
  3.1 0.0 copy-start.1
  3.1 0.8 %copy-done.1 = bf16[2,4,32,128]{3,2,1,0:T(8,128)(2,1)S(1)} copy-done((bf16[2,4,32,128]{3,2,1,0:T(8,128)(2,1)S(1)}, bf16[2,4,32,128]{3,2,1,0:T(8,128)(2,1)}, u32[]{:S(2)}) %copy-start.1) | copy-done | bytes 65560
  3.9 0.0 copy-start.2
  3.9 0.7 %copy-done.2 = f32[2,128]{1,0:T(2,128)S(1)} copy-done((f32[2,128]{1,0:T(2,128)S(1)}, f32[2,128]{1,0:T(2,128)}, u32[]{:S(2)}) %copy-start.2) | copy-done | bytes 1048
  4.6 44.1 %shard_map.68 = (bf16[2,4,32,128]{3,2,1,0:T(8,128)(2,1)S(1)}, f32[54,16,32]{2,1,0:T(8,128)S(1)}) custom-call(bf16[2,4,32,128]{3,2,1,0:T(8,128)(2,1)S(1)} %multiply_convert_fusion.x_in, bf16[2,27,128,128]{3,2,1,0:T(8,128)(2,1)S(1)} %copy-done, f32[2,128]{1,0:T(2,128)S(1)} %copy-done.2, bf16[2,4,32,128]{3,2,1,0:T(8,128)(2,1)S(1)} %copy-done.1), custom_call_target="tpu_custom_call" | custom-call | tf_op jit(solution)/shard_map/pallas_call | solution.py:346
  48.7 1.0 %copy.7 = f32[54,16,32]{0,2,1:T(8,128)} copy(f32[54,16,32]{2,1,0:T(8,128)S(1)} %broadcast_multiply_fusion) | data formatting | bytes 221184
  49.7 0.6 %copy.9 = bf16[2,4,32,128]{3,2,1,0:T(8,128)(2,1)} copy(bf16[2,4,32,128]{3,2,1,0:T(8,128)(2,1)S(1)} %get-tuple-element.10) | data formatting | bytes 131072
  (1 shorter events, 0.0 us)
Async XLA Ops:
  1.6 1.5 %copy-start = (bf16[2,27,128,128]{3,2,1,0:T(8,128)(2,1)S(1)}, bf16[2,27,128,128]{3,2,1,0:T(8,128)(2,1)}, u32[]{:S(2)}) copy-start(bf16[2,27,128,128]{3,2,1,0:T(8,128)(2,1)} %w_in.1) | copy-start | bytes 5308420
  3.1 0.8 %copy-start.1 = (bf16[2,4,32,128]{3,2,1,0:T(8,128)(2,1)S(1)}, bf16[2,4,32,128]{3,2,1,0:T(8,128)(2,1)}, u32[]{:S(2)}) copy-start(bf16[2,4,32,128]{3,2,1,0:T(8,128)(2,1)} %cot_in.1) | copy-start | bytes 196612
  3.9 0.7 %copy-start.2 = (f32[2,128]{1,0:T(2,128)S(1)}, f32[2,128]{1,0:T(2,128)}, u32[]{:S(2)}) copy-start(f32[2,128]{1,0:T(2,128)} %gains_ref.1) | copy-start | bytes 3076

commit v2 on v1

--- a/solution.py
+++ b/solution.py
@@ -20,7 +20,8 @@
 
 def kernel(
     sizes,
-    x_in,
+    codes_in,
+    scales_ref,
     w_in,
     gains_ref,
     cot_in,
@@ -30,6 +31,7 @@
     weights,
     turned,
     cot,
+    codes,
     patch,
     patch_back,
     z_keep,
@@ -62,13 +64,15 @@
     own_o = channels // nf
     group = -(-27 // nf)
 
-    x_copy = pltpu.make_async_copy(
-        x_in, ext.at[0, frames : 2 * frames, 1 : 1 + rows], local_sem.at[0]
-    )
+    x_copy = pltpu.make_async_copy(codes_in, codes, local_sem.at[0])
     w_copies = [
         pltpu.make_async_copy(w_in.at[l], weights.at[l], local_sem.at[1 + l]) for l in range(layers)
     ]
     cot_copy = pltpu.make_async_copy(cot_in, cot, local_sem.at[1 + layers])
+    x_copy.start()
+    for c in w_copies:
+        c.start()
+    cot_copy.start()
     for e in range(2 * layers):
         edge = jnp.zeros((2 * frames, 1, columns, channels), BF16)
         ext[e, :, 0:1] = edge
@@ -77,10 +81,6 @@
         ext[e, far : far + frames, 1 : 1 + rows] = jnp.zeros(
             (frames, rows, columns, channels), BF16
         )
-    x_copy.start()
-    for c in w_copies:
-        c.start()
-    cot_copy.start()
 
     offsets = {(0, 1), (0, nt - 1)}
     for df in (1, nf - 1):
@@ -99,6 +99,14 @@
             device_id=((f + df) % nf, (t + dt) % nt),
             device_id_type=MESH,
         )
+    x_copy.wait()
+    scales = scales_ref[...].reshape(frames * rows, columns).T
+    for i in range(frames):
+        for j in range(rows):
+            at = i * rows + j
+            ext[0, frames + i, 1 + j] = (codes[i, j].astype(F32) * scales[:, at : at + 1]).astype(
+                BF16
+            )
     pl.semaphore_wait(barrier, len(offsets))
 
     def halo(e):
@@ -255,7 +263,6 @@
                 ).reshape(group, own_q, channels)
             kg_ref[27 * l + low : 27 * l + high] = moved[: high - low, :, :own_o]
 
-    x_copy.wait()
     send_halo(0)
     for l in range(layers):
         total[l, 27:] = jnp.zeros((nf * group - 27, own_q, channels), F32)
@@ -298,9 +305,9 @@
         ext[e, 0:frames, 1 : 1 + rows] = pre_grad.reshape(frames, rows, columns, channels)
         send_halo(e)
         kernel_terms(l, pre_grad)
+        ring_stage(l)
         if l + 1 < layers:
             pack_stage(l + 1)
-        ring_stage(l)
         wait_halo(e)
         fill(patch_back, e)
         back = jnp.zeros((cells, channels), F32)
@@ -339,9 +346,8 @@
     pairs = nt // 2
     own_q, own_o = channels // nt, channels // nf
     group = -(-27 // nf)
-    layer_in = (saved_codes.astype(F32) * saved_scales[..., None]).astype(BF16)
     vmem = pl.BlockSpec(memory_space=pltpu.VMEM)
-    anywhere = pl.BlockSpec(memory_space=pl.ANY)
+    hbm = pl.BlockSpec(memory_space=pltpu.HBM)
     dma = pltpu.SemaphoreType.DMA
     input_grad, summed = pl.pallas_call(
         functools.partial(kernel, (nf, nt, layers, frames, rows, columns, channels)),
@@ -349,12 +355,13 @@
             jax.ShapeDtypeStruct((frames, rows, columns, channels), BF16),
             jax.ShapeDtypeStruct((27 * layers, own_q, own_o), F32),
         ),
-        in_specs=[anywhere, anywhere, vmem, anywhere],
+        in_specs=[hbm, vmem, hbm, vmem, hbm],
         out_specs=(vmem, vmem),
         scratch_shapes=[
             pltpu.VMEM((2 * layers, 2 * frames, rows + 2, columns, channels), BF16),
             pltpu.VMEM((layers, 27, channels, channels), BF16),
             pltpu.VMEM((layers, 3, 9 * channels, channels), BF16),
+            pltpu.VMEM((frames, rows, columns, channels), BF16),
             pltpu.VMEM((frames, rows, columns, channels), BF16),
             pltpu.VMEM((layers, 2 * cells, 9 * channels), BF16),
             pltpu.VMEM((2 * cells, 9 * channels), BF16),
@@ -377,9 +384,9 @@
             dma((layers, nf - 1)),
         ],
         compiler_params=pltpu.CompilerParams(
-            collective_id=0, has_side_effects=True, vmem_limit_bytes=50 * 1024 * 1024
+            collective_id=0, has_side_effects=True, vmem_limit_bytes=66_500_000
         ),
-    )(layer_in, kernels, norm_gains, cotangent)
+    )(saved_codes, saved_scales, kernels, norm_gains, cotangent)
     total_cells = cells * nf * nt
     return input_grad, summed / jnp.float32(math.sqrt(total_cells))
 

time: 50.6 us -> 48.9 us (0.966)
  local copies, waits for them, and re-layouts: 4.57 us -> 2.42 us
    unnamed x8 -> x2, local copies, waits for them, and re-layouts: 4.57 us -> 2.42 us
    div x1, other arithmetic: 0.04 us -> 1.05 us  [local(): return (input_grad, summed / jnp.float32(math.sqrt(total_cells)))]
    convert_element_type x1 -> x0, other arithmetic: 0.94 us -> none  [local(): layer_in = (saved_codes.astype(F32) * saved_scales[..., None]).astype(BF16)]
where the time goes in v2:
time: 48.9 us; the launch traced here: 48.7 us
  Pallas kernels  44.5 us (91%)
  local copies, waits for them, and re-layouts  2.42 us (5%)
  other arithmetic  1.05 us (2%)
  between operations  0.64 us (1%)
    pallas_call x1, Pallas kernels, local(): pl.pallas_call(functools.partial(kernel, (nf, nt, layers, frames, rows, c...  44.5 us
    unnamed x2, local copies, waits for them, and re-layouts  2.42 us
    div x1, other arithmetic, local(): return (input_grad, summed / jnp.float32(math.sqrt(total_cells)))  1.05 us

profile of v2, /device:TPU:0, one launch (start us, length us, event | category | flops | bytes accessed | tf_op | source)
XLA Modules:
  0.0 48.7 jit_solution(3878119304360834320)
XLA Ops:
  0.6 44.5 %shard_map.68 = (bf16[2,4,32,128]{3,2,1,0:T(8,128)(2,1)}, f32[54,16,32]{2,1,0:T(8,128)}) custom-call(bf16[2,4,32,128]{3,2,1,0:T(8,128)(2,1)} %codes_in.1, f32[2,4,32]{2,1,0:T(4,128)} %scales_ref.1, bf16[2,27,128,128]{3,2,1,0:T(8,128)(2,1)} %w_in.1, f32[2,128]{1,0:T(2,128)} %gains_ref.1, bf16[2,4,32,128]{3,2,1,0:T(8,128)(2,1)} %cot_in.1), custom_call_target="tpu_custom_call" | custom-call | tf_op jit(solution)/shard_map/pallas_call | solution.py:352
  45.2 1.1 %broadcast_multiply_fusion = f32[54,16,32]{2,1,0:T(8,128)S(1)} fusion(f32[54,16,32]{2,1,0:T(8,128)} %get-tuple-element.5), kind=kLoop, calls=%fused_computation | loop fusion | flops 27648 | bytes 221184 | tf_op jit(solution)/shard_map/div | solution.py:391
  46.2 1.0 %copy.7 = f32[54,16,32]{0,2,1:T(8,128)} copy(f32[54,16,32]{2,1,0:T(8,128)S(1)} %broadcast_multiply_fusion) | data formatting | bytes 221184
  47.2 1.5 %copy.9 = bf16[2,4,32,128]{3,2,1,0:T(8,128)(2,1)} copy(bf16[2,4,32,128]{3,2,1,0:T(8,128)(2,1)} %get-tuple-element.10) | data formatting | bytes 131072

commit v3 on v2

--- a/solution.py
+++ b/solution.py
@@ -35,6 +35,7 @@
     patch,
     patch_back,
     z_keep,
+    terms,
     pair_out,
     pair_in,
     ring_out,
@@ -42,6 +43,13 @@
     total,
     pack_out,
     pack_in,
+    wide_pair_out,
+    wide_pair_in,
+    wide_frame_out,
+    wide_frame_in,
+    wide_total,
+    wide_ring_out,
+    wide_ring_in,
     local_sem,
     halo_send,
     halo_recv,
@@ -51,6 +59,12 @@
     ring_recv,
     pack_send,
     pack_recv,
+    wide_pair_send,
+    wide_pair_recv,
+    wide_frame_send,
+    wide_frame_recv,
+    wide_ring_send,
+    wide_ring_recv,
 ):
     nf, nt, layers, frames, rows, columns, channels = sizes
     f = lax.axis_index("frame")
@@ -62,7 +76,7 @@
     cells = frames * block
     own_q = channels // nt
     own_o = channels // nf
-    group = -(-27 // nf)
+    group, wide = -(-9 // nf), -(-18 // nf)
 
     x_copy = pltpu.make_async_copy(codes_in, codes, local_sem.at[0])
     w_copies = [
@@ -166,106 +180,181 @@
             a, m = k // 9, 8 - k % 9
             turned[l, a, m * channels : (m + 1) * channels, :] = weights[l, k].T
 
-    def pair_copy(l, a):
+    def remote(source, target, sends, recvs, device):
         return pltpu.make_async_remote_copy(
-            src_ref=pair_out.at[l, a, 1 - core],
-            dst_ref=pair_in.at[l, a],
-            send_sem=pair_send.at[l, a],
-            recv_sem=pair_recv.at[l, a],
-            device_id=(f, t + 1 - 2 * core),
+            src_ref=source,
+            dst_ref=target,
+            send_sem=sends,
+            recv_sem=recvs,
+            device_id=device,
             device_id_type=MESH,
         )
 
-    def ring_copy(l, a, s):
+    partner = (f, t + 1 - 2 * core)
+
+    def pair_copy(l):
+        return remote(
+            pair_out.at[l, 1 - core], pair_in.at[l], pair_send.at[l], pair_recv.at[l], partner
+        )
+
+    def ring_copy(l, s):
         peer = (place + s) % pairs
-        return pltpu.make_async_remote_copy(
-            src_ref=ring_out.at[l, a, peer],
-            dst_ref=ring_in.at[l, a, s - 1],
-            send_sem=ring_send.at[l, a, s - 1],
-            recv_sem=ring_recv.at[l, a, s - 1],
-            device_id=(f, 2 * peer + core),
-            device_id_type=MESH,
+        return remote(
+            ring_out.at[l, peer],
+            ring_in.at[l, s - 1],
+            ring_send.at[l, s - 1],
+            ring_recv.at[l, s - 1],
+            (f, 2 * peer + core),
         )
 
     def pack_copy(l, s):
         peer = (f + s) % nf
-        return pltpu.make_async_remote_copy(
-            src_ref=pack_out.at[l, peer],
-            dst_ref=pack_in.at[l, s - 1],
-            send_sem=pack_send.at[l, s - 1],
-            recv_sem=pack_recv.at[l, s - 1],
-            device_id=(peer, t),
-            device_id_type=MESH,
-        )
-
-    def kernel_terms(l, pre_grad):
-        for a in range(3):
-            part = lax.dot_general(
-                patch[l, a * block : a * block + cells, :],
-                pre_grad,
-                (((0,), (0,)), ((), ())),
-                preferred_element_type=F32,
-            )
-            part = part.astype(BF16).reshape(9, channels, channels)
-            for d in range(nt):
-                pair_out[l, a, d % 2, d // 2] = part[:, d * own_q : (d + 1) * own_q]
-            pair_copy(l, a).start()
-
-    def ring_stage(l):
-        for a in range(3):
-            pair_copy(l, a).wait_recv()
-            for s in range(1, pairs):
-                peer = (place + s) % pairs
-                ring_out[l, a, peer] = (
-                    pair_out[l, a, core, peer].astype(F32) + pair_in[l, a, peer].astype(F32)
-                ).astype(BF16)
-                ring_copy(l, a, s).start()
-            total[l, 9 * a : 9 * a + 9] = pair_out[l, a, core, place].astype(F32) + pair_in[
-                l, a, place
-            ].astype(F32)
-
-    lane_block = lax.broadcasted_iota(jnp.int32, (group, own_q, channels), 2) // own_o
-
-    def pack_stage(l):
-        for a in range(3):
-            value = total[l, 9 * a : 9 * a + 9]
-            for s in range(1, pairs):
-                ring_copy(l, a, s).wait_recv()
-                value = value + ring_in[l, a, s - 1].astype(F32)
-            total[l, 9 * a : 9 * a + 9] = value
-        for d in range(nf):
-            packed = jnp.zeros((group, own_q, channels), F32)
-            for j in range(nf):
-                piece = total[l, j * group : (j + 1) * group]
-                shift = ((j - d) * own_o) % channels
-                if shift:
-                    piece = pltpu.roll(
-                        piece.reshape(group * own_q, channels), shift, 1
-                    ).reshape(group, own_q, channels)
-                packed = jnp.where(lane_block == j, piece, packed)
-            pack_out[l, d] = packed.astype(BF16)
-        for s in range(1, nf):
-            pack_copy(l, s).start()
-
-    def finish(l):
-        value = pack_out[l, f].astype(F32)
-        for s in range(1, nf):
-            pack_copy(l, s).wait_recv()
-            value = value + pack_in[l, s - 1].astype(F32)
+        return remote(
+            pack_out.at[l, peer],
+            pack_in.at[l, s - 1],
+            pack_send.at[l, s - 1],
+            pack_recv.at[l, s - 1],
+            (peer, t),
+        )
+
+    def wide_pair_copy(l, d):
+        return remote(
+            wide_pair_out.at[l, d, 1 - core],
+            wide_pair_in.at[l, d],
+            wide_pair_send.at[l, d],
+            wide_pair_recv.at[l, d],
+            partner,
+        )
+
+    def wide_frame_copy(l, s):
+        peer = (f + s) % nf
+        return remote(
+            wide_frame_out.at[l, peer],
+            wide_frame_in.at[l, s - 1],
+            wide_frame_send.at[l, s - 1],
+            wide_frame_recv.at[l, s - 1],
+            (peer, t),
+        )
+
+    def wide_ring_copy(l, s):
+        peer = (place + s) % pairs
+        return remote(
+            wide_ring_out.at[l, peer],
+            wide_ring_in.at[l, s - 1],
+            wide_ring_send.at[l, s - 1],
+            wide_ring_recv.at[l, s - 1],
+            (f, 2 * peer + core),
+        )
+
+    def packed(source, size, d):
+        height = source.shape[1]
+        lane_block = lax.broadcasted_iota(jnp.int32, (size * height, channels), 1) // own_o
+        result = jnp.zeros((size * height, channels), F32)
         for j in range(nf):
-            low, high = j * group, min(27, (j + 1) * group)
+            piece = source[j * size : (j + 1) * size].reshape(size * height, channels)
+            shift = ((j - d) * own_o) % channels
+            if shift:
+                piece = pltpu.roll(piece, shift, 1)
+            result = jnp.where(lane_block == j, piece, result)
+        return result.reshape(size, height, channels)
+
+    def unpack(value, size, first, count):
+        for j in range(nf):
+            low, high = j * size, min(count, (j + 1) * size)
             if low >= high:
                 break
             moved = value
             if j:
                 moved = pltpu.roll(
-                    value.reshape(group * own_q, channels), channels - j * own_o, 1
-                ).reshape(group, own_q, channels)
-            kg_ref[27 * l + low : 27 * l + high] = moved[: high - low, :, :own_o]
-
+                    value.reshape(size * own_q, channels), channels - j * own_o, 1
+                ).reshape(size, own_q, channels)
+            kg_ref[first + low : first + high] = moved[: high - low, :, :own_o]
+
+    def kernel_term(l, a, pre_grad):
+        part = lax.dot_general(
+            patch[l, a * block : a * block + cells, :],
+            pre_grad,
+            (((0,), (0,)), ((), ())),
+            preferred_element_type=F32,
+        )
+        return part.reshape(9, channels, channels)
+
+    def kernel_terms(l, pre_grad):
+        for a in (1, 2):
+            terms[9 * a - 9 : 9 * a] = kernel_term(l, a, pre_grad)
+        for d in range(nf):
+            part = packed(terms, wide, d).astype(BF16)
+            for q in range(nt):
+                wide_pair_out[l, d, q % 2, q // 2] = part[:, q * own_q : (q + 1) * own_q]
+            wide_pair_copy(l, d).start()
+        part = kernel_term(l, 0, pre_grad).astype(BF16)
+        for q in range(nt):
+            pair_out[l, q % 2, q // 2] = part[:, q * own_q : (q + 1) * own_q]
+        pair_copy(l).start()
+
+    def ring_stage(l):
+        for s in range(1, nf):
+            peer = (f + s) % nf
+            wide_pair_copy(l, peer).wait_recv()
+            wide_frame_out[l, peer] = (
+                wide_pair_out[l, peer, core].astype(F32) + wide_pair_in[l, peer].astype(F32)
+            ).astype(BF16)
+            wide_frame_copy(l, s).start()
+        pair_copy(l).wait_recv()
+        for s in range(1, pairs):
+            peer = (place + s) % pairs
+            ring_out[l, peer] = (
+                pair_out[l, core, peer].astype(F32) + pair_in[l, peer].astype(F32)
+            ).astype(BF16)
+            ring_copy(l, s).start()
+        total[l, 0:9] = pair_out[l, core, place].astype(F32) + pair_in[l, place].astype(F32)
+        wide_pair_copy(l, f).wait_recv()
+        wide_total[l] = wide_pair_out[l, f, core].astype(F32) + wide_pair_in[l, f].astype(F32)
+
+    def pack_stage(l):
+        for s in range(1, nf):
+            wide_frame_copy(l, s).wait_recv()
+
+        def wide_sum(p):
+            value = wide_total[l, p]
+            for s in range(1, nf):
+                value = value + wide_frame_in[l, s - 1, p].astype(F32)
+            return value
+
+        for s in range(1, pairs):
+            peer = (place + s) % pairs
+            wide_ring_out[l, peer] = wide_sum(peer).astype(BF16)
+            wide_ring_copy(l, s).start()
+        wide_total[l, place] = wide_sum(place)
+        value = total[l, 0:9]
+        for s in range(1, pairs):
+            ring_copy(l, s).wait_recv()
+            value = value + ring_in[l, s - 1].astype(F32)
+        total[l, 0:9] = value
+        for d in range(nf):
+            pack_out[l, d] = packed(total.at[l], group, d).astype(BF16)
+        for s in range(1, nf):
+            pack_copy(l, s).start()
+
+    def finish(l):
+        value = wide_total[l, place]
+        for s in range(1, pairs):
+            wide_ring_copy(l, s).wait_recv()
+            value = value + wide_ring_in[l, s - 1].astype(F32)
+        unpack(value * scale, wide, 27 * l + 9, 18)
+        value = pack_out[l, f].astype(F32)
+        for s in range(1, nf):
+            pack_copy(l, s).wait_recv()
+            value = value + pack_in[l, s - 1].astype(F32)
+        unpack(value * scale, group, 27 * l, 9)
+
+    scale = 1.0 / math.sqrt(cells * nf * nt)
     send_halo(0)
     for l in range(layers):
-        total[l, 27:] = jnp.zeros((nf * group - 27, own_q, channels), F32)
+        if nf * group > 9:
+            total[l, 9:] = jnp.zeros((nf * group - 9, own_q, channels), F32)
+    if nf * wide > 18:
+        terms[18:] = jnp.zeros((nf * wide - 18, channels, channels), F32)
     for l in range(layers):
         w_copies[l].wait()
         if l == 0:
@@ -328,12 +417,15 @@
         for copy, can_send, _ in halos[e]:
             pl.when(can_send)(copy.wait_send)
     for l in range(layers):
-        for a in range(3):
-            pair_copy(l, a).wait_send()
-            for s in range(1, pairs):
-                ring_copy(l, a, s).wait_send()
+        pair_copy(l).wait_send()
+        for d in range(nf):
+            wide_pair_copy(l, d).wait_send()
+        for s in range(1, pairs):
+            ring_copy(l, s).wait_send()
+            wide_ring_copy(l, s).wait_send()
         for s in range(1, nf):
             pack_copy(l, s).wait_send()
+            wide_frame_copy(l, s).wait_send()
 
 
 def local(saved_codes, saved_scales, kernels, norm_gains, cotangent):
@@ -345,7 +437,7 @@
     cells = frames * block
     pairs = nt // 2
     own_q, own_o = channels // nt, channels // nf
-    group = -(-27 // nf)
+    group, wide = -(-9 // nf), -(-18 // nf)
     vmem = pl.BlockSpec(memory_space=pltpu.VMEM)
     hbm = pl.BlockSpec(memory_space=pltpu.HBM)
     dma = pltpu.SemaphoreType.DMA
@@ -366,29 +458,42 @@
             pltpu.VMEM((layers, 2 * cells, 9 * channels), BF16),
             pltpu.VMEM((2 * cells, 9 * channels), BF16),
             pltpu.VMEM((layers, cells, channels), F32),
-            pltpu.VMEM((layers, 3, 2, pairs, 9, own_q, channels), BF16),
-            pltpu.VMEM((layers, 3, pairs, 9, own_q, channels), BF16),
-            pltpu.VMEM((layers, 3, pairs, 9, own_q, channels), BF16),
-            pltpu.VMEM((layers, 3, pairs - 1, 9, own_q, channels), BF16),
+            pltpu.VMEM((nf * wide, channels, channels), F32),
+            pltpu.VMEM((layers, 2, pairs, 9, own_q, channels), BF16),
+            pltpu.VMEM((layers, pairs, 9, own_q, channels), BF16),
+            pltpu.VMEM((layers, pairs, 9, own_q, channels), BF16),
+            pltpu.VMEM((layers, pairs - 1, 9, own_q, channels), BF16),
             pltpu.VMEM((layers, nf * group, own_q, channels), F32),
             pltpu.VMEM((layers, nf, group, own_q, channels), BF16),
             pltpu.VMEM((layers, nf - 1, group, own_q, channels), BF16),
+            pltpu.VMEM((layers, nf, 2, pairs, wide, own_q, channels), BF16),
+            pltpu.VMEM((layers, nf, pairs, wide, own_q, channels), BF16),
+            pltpu.VMEM((layers, nf, pairs, wide, own_q, channels), BF16),
+            pltpu.VMEM((layers, nf - 1, pairs, wide, own_q, channels), BF16),
+            pltpu.VMEM((layers, pairs, wide, own_q, channels), F32),
+            pltpu.VMEM((layers, pairs, wide, own_q, channels), BF16),
+            pltpu.VMEM((layers, pairs - 1, wide, own_q, channels), BF16),
             dma((2 + layers,)),
             dma((2 * layers, 5)),
             dma((2 * layers, 5)),
-            dma((layers, 3)),
-            dma((layers, 3)),
-            dma((layers, 3, pairs - 1)),
-            dma((layers, 3, pairs - 1)),
+            dma((layers,)),
+            dma((layers,)),
+            dma((layers, pairs - 1)),
+            dma((layers, pairs - 1)),
             dma((layers, nf - 1)),
             dma((layers, nf - 1)),
+            dma((layers, nf)),
+            dma((layers, nf)),
+            dma((layers, nf - 1)),
+            dma((layers, nf - 1)),
+            dma((layers, pairs - 1)),
+            dma((layers, pairs - 1)),
         ],
         compiler_params=pltpu.CompilerParams(
-            collective_id=0, has_side_effects=True, vmem_limit_bytes=66_500_000
+            collective_id=0, has_side_effects=True, vmem_limit_bytes=65_700_000
         ),
     )(saved_codes, saved_scales, kernels, norm_gains, cotangent)
-    total_cells = cells * nf * nt
-    return input_grad, summed / jnp.float32(math.sqrt(total_cells))
+    return input_grad, summed
 
 
 def solution(mesh):

time: 48.9 us -> 41.1 us (0.84)
  Pallas kernels: 44.5 us -> 36.8 us
  other arithmetic: 1.05 us -> 0 us
  local copies, waits for them, and re-layouts: 2.42 us -> 3.42 us
    pallas_call x1, Pallas kernels: 44.5 us -> 36.8 us  [local(): pl.pallas_call(functools.partial(kernel, (nf, nt, layers, frames, rows, c...]
    pallas_call x0 -> x1, local copies, waits for them, and re-layouts: none -> 1.95 us  [local(): pl.pallas_call(functools.partial(kernel, (nf, nt, layers, frames, rows, c...]
    div x1 -> x0, other arithmetic: 1.05 us -> none  [local(): return (input_grad, summed / jnp.float32(math.sqrt(total_cells)))]
    unnamed x2 -> x1, local copies, waits for them, and re-layouts: 2.42 us -> 1.47 us
where the time goes in v3:
time: 41.1 us; the launch traced here: 40.9 us
  Pallas kernels  36.8 us (90%)
  local copies, waits for them, and re-layouts  3.42 us (8%)
  between operations  0.64 us (2%)
    pallas_call x1, Pallas kernels, local(): pl.pallas_call(functools.partial(kernel, (nf, nt, layers, frames, rows, c...  36.8 us
    pallas_call x1, local copies, waits for them, and re-layouts, local(): pl.pallas_call(functools.partial(kernel, (nf, nt, layers, frames, rows, c...  1.95 us
    unnamed x1, local copies, waits for them, and re-layouts  1.47 us

profile of v3, /device:TPU:0, one launch (start us, length us, event | category | flops | bytes accessed | tf_op | source)
XLA Modules:
  0.0 40.9 jit_solution(8138604515060266577)
XLA Ops:
  0.6 36.8 %shard_map.68 = (bf16[2,4,32,128]{3,2,1,0:T(8,128)(2,1)}, f32[54,16,32]{2,1,0:T(8,128)}) custom-call(bf16[2,4,32,128]{3,2,1,0:T(8,128)(2,1)} %codes_in.1, f32[2,4,32]{2,1,0:T(4,128)} %scales_ref.1, bf16[2,27,128,128]{3,2,1,0:T(8,128)(2,1)} %w_in.1, f32[2,128]{1,0:T(2,128)} %gains_ref.1, bf16[2,4,32,128]{3,2,1,0:T(8,128)(2,1)} %cot_in.1), custom_call_target="tpu_custom_call" | custom-call | tf_op jit(solution)/shard_map/pallas_call | solution.py:444
  37.4 1.9 %copy.7 = f32[54,16,32]{0,2,1:T(8,128)} copy(f32[54,16,32]{2,1,0:T(8,128)} %get-tuple-element.3) | data formatting | bytes 221184 | tf_op jit(solution)/shard_map/pallas_call | solution.py:444
  39.4 1.5 %copy.9 = bf16[2,4,32,128]{3,2,1,0:T(8,128)(2,1)} copy(bf16[2,4,32,128]{3,2,1,0:T(8,128)(2,1)} %get-tuple-element.6) | data formatting | bytes 131072

commit v4 on v3

--- a/solution.py
+++ b/solution.py
@@ -35,6 +35,7 @@
     patch,
     patch_back,
     z_keep,
+    summed,
     terms,
     pair_out,
     pair_in,
@@ -156,24 +157,54 @@
         for copy, can_send, _ in halos[e]:
             pl.when(can_send)(copy.start)
 
-    def wait_halo(e):
-        for copy, _, can_recv in halos[e]:
+    def wait_halo(e, indices):
+        for index in indices:
+            copy, _, can_recv = halos[e][index]
             pl.when(can_recv)(copy.wait_recv)
 
-    height = 2 * frames * (rows + 2) * columns
+    height = frames * (rows + 2) * columns
     column = lax.broadcasted_iota(jnp.int32, (height, channels), 0) % columns
 
-    def fill(target, e):
-        flat = ext[e].astype(F32).reshape(height, channels)
+    def fill(target, e, first):
+        part = ext[e, first : first + frames].reshape(height, channels)
+        flat = part.astype(F32)
         before = jnp.where(column == 0, 0.0, pltpu.roll(flat, 1, 0)).astype(BF16)
         after = jnp.where(column == columns - 1, 0.0, pltpu.roll(flat, height - 1, 0)).astype(BF16)
-        for c, value in enumerate((before, ext[e].reshape(height, channels), after)):
-            value = value.reshape(2 * frames, rows + 2, columns, channels)
+        low = first * block
+        for c, value in enumerate((before, part, after)):
+            value = value.reshape(frames, rows + 2, columns, channels)
             for b in range(3):
                 at = (3 * b + c) * channels
-                target[:, at : at + channels] = value[:, b : b + rows].reshape(
-                    2 * cells, channels
+                target[low : low + cells, at : at + channels] = value[:, b : b + rows].reshape(
+                    cells, channels
                 )
+
+    def convolve(target, e, weight):
+        forward = e < layers
+        own, far = (frames, 0) if forward else (0, frames)
+
+        def product(low, high, order):
+            return jnp.dot(
+                target[low * block : high * block, :],
+                weight(order if forward else 2 - order),
+                preferred_element_type=F32,
+            )
+
+        wait_halo(e, (1, 2))
+        fill(target, e, own)
+        if forward:
+            summed[...] = product(2, 4, 2)
+            summed[block:cells] += product(2, 3, 1)
+        else:
+            summed[...] = product(0, 2, 0)
+            summed[0:block] += product(1, 2, 1)
+        wait_halo(e, (0, 3, 4))
+        fill(target, e, far)
+        if forward:
+            summed[0:block] += product(1, 2, 1)
+            return summed[...] + product(0, 2, 0)
+        summed[block:cells] += product(2, 3, 1)
+        return summed[...] + product(2, 4, 2)
 
     def turn(l):
         for k in range(27):
@@ -361,15 +392,11 @@
             turn(layers - 1 if layers == 1 else 0)
         else:
             turn(l)
-        wait_halo(l)
-        fill(patch.at[l], l)
-        z = jnp.zeros((cells, channels), F32)
-        for a in range(3):
-            z = z + jnp.dot(
-                patch[l, a * block : a * block + cells, :],
-                weights[l, 9 * a : 9 * a + 9].reshape(9 * channels, channels),
-                preferred_element_type=F32,
-            )
+        z = convolve(
+            patch.at[l],
+            l,
+            lambda a: weights[l, 9 * a : 9 * a + 9].reshape(9 * channels, channels),
+        )
         z_keep[l] = z
         if l + 1 < layers:
             inverse = lax.rsqrt(jnp.mean(z * z, axis=-1, keepdims=True) + EPS)
@@ -394,17 +421,10 @@
         ext[e, 0:frames, 1 : 1 + rows] = pre_grad.reshape(frames, rows, columns, channels)
         send_halo(e)
         kernel_terms(l, pre_grad)
-        ring_stage(l)
         if l + 1 < layers:
             pack_stage(l + 1)
-        wait_halo(e)
-        fill(patch_back, e)
-        back = jnp.zeros((cells, channels), F32)
-        for a in range(3):
-            start = (2 - a) * block
-            back = back + jnp.dot(
-                patch_back[start : start + cells, :], turned[l, a], preferred_element_type=F32
-            )
+        ring_stage(l)
+        back = convolve(patch_back, e, lambda a: turned[l, a])
         back = back.astype(BF16)
         upstream = back.astype(F32)
         if l + 1 < layers:
@@ -458,6 +478,7 @@
             pltpu.VMEM((layers, 2 * cells, 9 * channels), BF16),
             pltpu.VMEM((2 * cells, 9 * channels), BF16),
             pltpu.VMEM((layers, cells, channels), F32),
+            pltpu.VMEM((cells, channels), F32),
             pltpu.VMEM((nf * wide, channels, channels), F32),
             pltpu.VMEM((layers, 2, pairs, 9, own_q, channels), BF16),
             pltpu.VMEM((layers, pairs, 9, own_q, channels), BF16),

time: 41.1 us -> 40.3 us (0.981)
  Pallas kernels: 36.8 us -> 35.9 us
    pallas_call x1, Pallas kernels: 36.8 us -> 35.9 us  [local(): pl.pallas_call(functools.partial(kernel, (nf, nt, layers, frames, rows, c...]
where the time goes in v4:
time: 40.3 us; the launch traced here: 40 us
  Pallas kernels  35.9 us (89%)
  local copies, waits for them, and re-layouts  3.42 us (8%)
  between operations  0.64 us (2%)
    pallas_call x1, Pallas kernels, local(): pl.pallas_call(functools.partial(kernel, (nf, nt, layers, frames, rows, c...  35.9 us
    pallas_call x1, local copies, waits for them, and re-layouts, local(): pl.pallas_call(functools.partial(kernel, (nf, nt, layers, frames, rows, c...  1.95 us
    unnamed x1, local copies, waits for them, and re-layouts  1.47 us

profile of v4, /device:TPU:0, one launch (start us, length us, event | category | flops | bytes accessed | tf_op | source)
XLA Modules:
  0.0 40.0 jit_solution(6578772545198048021)
XLA Ops:
  0.6 35.9 %shard_map.68 = (bf16[2,4,32,128]{3,2,1,0:T(8,128)(2,1)}, f32[54,16,32]{2,1,0:T(8,128)}) custom-call(bf16[2,4,32,128]{3,2,1,0:T(8,128)(2,1)} %codes_in.1, f32[2,4,32]{2,1,0:T(4,128)} %scales_ref.1, bf16[2,27,128,128]{3,2,1,0:T(8,128)(2,1)} %w_in.1, f32[2,128]{1,0:T(2,128)} %gains_ref.1, bf16[2,4,32,128]{3,2,1,0:T(8,128)(2,1)} %cot_in.1), custom_call_target="tpu_custom_call" | custom-call | tf_op jit(solution)/shard_map/pallas_call | solution.py:464
  36.6 1.9 %copy.7 = f32[54,16,32]{0,2,1:T(8,128)} copy(f32[54,16,32]{2,1,0:T(8,128)} %get-tuple-element.3) | data formatting | bytes 221184 | tf_op jit(solution)/shard_map/pallas_call | solution.py:464
  38.5 1.5 %copy.9 = bf16[2,4,32,128]{3,2,1,0:T(8,128)(2,1)} copy(bf16[2,4,32,128]{3,2,1,0:T(8,128)(2,1)} %get-tuple-element.6) | data formatting | bytes 131072

commit v5 on v4

--- a/solution.py
+++ b/solution.py
@@ -464,8 +464,8 @@
     input_grad, summed = pl.pallas_call(
         functools.partial(kernel, (nf, nt, layers, frames, rows, columns, channels)),
         out_shape=(
-            jax.ShapeDtypeStruct((frames, rows, columns, channels), BF16),
-            jax.ShapeDtypeStruct((27 * layers, own_q, own_o), F32),
+            pltpu.VMEM((frames, rows, columns, channels), BF16),
+            pltpu.VMEM((27 * layers, own_q, own_o), F32),
         ),
         in_specs=[hbm, vmem, hbm, vmem, hbm],
         out_specs=(vmem, vmem),
@@ -511,7 +511,7 @@
             dma((layers, pairs - 1)),
         ],
         compiler_params=pltpu.CompilerParams(
-            collective_id=0, has_side_effects=True, vmem_limit_bytes=65_700_000
+            collective_id=0, has_side_effects=True, vmem_limit_bytes=62_000_000
         ),
     )(saved_codes, saved_scales, kernels, norm_gains, cotangent)
     return input_grad, summed

time: 40.3 us -> 37.6 us (0.933)
  local copies, waits for them, and re-layouts: 3.42 us -> 1.58 us
  Pallas kernels: 35.9 us -> 35.2 us
    pallas_call x1, local copies, waits for them, and re-layouts: 1.95 us -> 0.95 us  [local(): pl.pallas_call(functools.partial(kernel, (nf, nt, layers, frames, rows, c...]
    unnamed x1, local copies, waits for them, and re-layouts: 1.47 us -> 0.63 us
    pallas_call x1, Pallas kernels: 35.9 us -> 35.2 us  [local(): pl.pallas_call(functools.partial(kernel, (nf, nt, layers, frames, rows, c...]
where the time goes in v5:
time: 37.6 us; the launch traced here: 37.4 us
  Pallas kernels  35.2 us (94%)
  local copies, waits for them, and re-layouts  1.58 us (4%)
  between operations  0.64 us (2%)
    pallas_call x1, Pallas kernels, local(): pl.pallas_call(functools.partial(kernel, (nf, nt, layers, frames, rows, c...  35.2 us
    pallas_call x1, local copies, waits for them, and re-layouts, local(): pl.pallas_call(functools.partial(kernel, (nf, nt, layers, frames, rows, c...  0.95 us

profile of v5, /device:TPU:0, one launch (start us, length us, event | category | flops | bytes accessed | tf_op | source)
XLA Modules:
  0.0 37.4 jit_solution(16858602346921273780)
XLA Ops:
  0.6 35.2 %shard_map.68 = (bf16[2,4,32,128]{3,2,1,0:T(8,128)(2,1)S(1)}, f32[54,16,32]{2,1,0:T(8,128)S(1)}) custom-call(bf16[2,4,32,128]{3,2,1,0:T(8,128)(2,1)} %codes_in.1, f32[2,4,32]{2,1,0:T(4,128)} %scales_ref.1, bf16[2,27,128,128]{3,2,1,0:T(8,128)(2,1)} %w_in.1, f32[2,128]{1,0:T(2,128)} %gains_ref.1, bf16[2,4,32,128]{3,2,1,0:T(8,128)(2,1)} %cot_in.1), custom_call_target="tpu_custom_call" | custom-call | tf_op jit(solution)/shard_map/pallas_call | solution.py:464
  35.8 0.6 %copy.9 = bf16[2,4,32,128]{3,2,1,0:T(8,128)(2,1)} copy(bf16[2,4,32,128]{3,2,1,0:T(8,128)(2,1)S(1)} %get-tuple-element.4) | data formatting | bytes 131072
  36.4 0.9 %copy.7 = f32[54,16,32]{0,2,1:T(8,128)} copy(f32[54,16,32]{2,1,0:T(8,128)S(1)} %get-tuple-element.3) | data formatting | bytes 221184 | tf_op jit(solution)/shard_map/pallas_call | solution.py:464
